TPU v7x, 32 devices: a whole 2x2x4 slice. The times are simulated.
32 devices in a mesh: groups: 2 (over y), space: 4 (over z), freq: 2 (over x), band: 2 (over core).
Axes of the slice: x: 2, y: 2, z: 4, core: 2. Of those that a mesh axis runs over, the one named last changes fastest.
Arguments:
- snapshots: bfloat16 [16, 256, 32768], P(('freq', 'band'), None, ('groups', 'space')), parts along dimension 2, may hold values from -6 to 6
- weights: float32 [32768], P(('groups', 'space')), parts along dimension 0, may hold values from 0.25 to 2.5
- triads: int32 [64, 2], replicated, may hold values from 0 to 63, as said below
Outputs:
- bispectra: float32 [128, 512], P(('groups', 'space', 'freq', 'band')), parts along dimension 0
There are 2 independent parts, one for each index of `groups`. A program takes and returns all parts, laid end to end along the dimension named above; an argument that names none is the same for every part. Nothing has to cross between parts.
Inputs may be any that keep to these rules, and one draw needn't show every extreme that they name: `triads`: each row is a pair (k, l) with k >= l and k + l <= 63; all pairs are distinct; the pair (63, 0) is always present.
All inputs are finite; a program needn't handle non-finite values.
Results may differ from a plain program's by a relative error of at most 0.0078.
Values may be sent and summed in bfloat16 or wider, within the bound.
No kernel may reach another device: no remote copies, remote signals or barrier semaphores. Data moves between devices by JAX's collectives and lax.ppermute only.
A program may use at most 128 MiB of HBM per device.

v0:
```python
import math
import jax
import jax.numpy as jnp
from jax import lax
from jax.sharding import PartitionSpec as P

NB = 16
NF = 64


def make_table(length):
    time_steps = jnp.arange(length, dtype=jnp.int32)
    frequency = jnp.arange(NF, dtype=jnp.int32)
    phase_index = frequency[:, None] * time_steps[None, :] % length
    angle_grid = phase_index.astype(jnp.float32) * (2.0 * math.pi / length)
    hann_window = 0.5 - 0.5 * jnp.cos(time_steps.astype(jnp.float32) * (2.0 * math.pi / length))
    gain_factor = 1.0 / math.sqrt(3.0 * length / 8.0)
    cos_rows = hann_window[None, :] * jnp.cos(angle_grid) * gain_factor
    sin_rows = -hann_window[None, :] * jnp.sin(angle_grid) * gain_factor
    return jnp.concatenate([cos_rows, sin_rows], axis=0).astype(jnp.bfloat16)


def triad_block(spectra_grid, weights, triad_block_ids):
    first_freq = triad_block_ids[:, 0]
    second_freq = triad_block_ids[:, 1]
    third_freq = first_freq + second_freq
    first_spec = jnp.take(spectra_grid, first_freq, axis=2).astype(jnp.float32)
    second_spec = jnp.take(spectra_grid, second_freq, axis=2).astype(jnp.float32)
    third_spec = jnp.take(spectra_grid, third_freq, axis=2)
    prod_re = weights * (
        first_spec[:, 0] * second_spec[:, 0] - first_spec[:, 1] * second_spec[:, 1]
    )
    prod_im = weights * (
        first_spec[:, 0] * second_spec[:, 1] + first_spec[:, 1] * second_spec[:, 0]
    )
    field_a = jnp.stack([prod_re, prod_im], axis=1).astype(jnp.bfloat16)
    products = jnp.einsum(
        "ictx,jdtx->tcdij", field_a, third_spec, preferred_element_type=jnp.float32
    )
    real_part = products[:, 0, 0] + products[:, 1, 1]
    imag_part = products[:, 0, 1] - products[:, 1, 0]
    stacked = jnp.stack([real_part, imag_part], axis=1)
    return stacked.reshape(triad_block_ids.shape[0], 2 * NB * NB)


def block_terms(spectra, weights, triad_rows, point_scale):
    row_count = triad_rows.shape[0]
    columns = spectra.shape[2]
    spectra_grid = spectra.reshape(NB, 2, NF, columns)
    block_size = math.gcd(row_count, max(1, 32768 // columns))
    grouped = triad_rows.reshape(row_count // block_size, block_size, 2)

    def one_group(triad_block_ids):
        return triad_block(spectra_grid, weights, triad_block_ids) * point_scale

    result = lax.map(one_group, grouped)
    return result.reshape(row_count, 2 * NB * NB)


def per_device(snapshots, weights, triads):
    local_blocks, length, points = snapshots.shape
    dft_table = make_table(length)
    spec_local = jnp.einsum(
        "ct,btx->bcx", dft_table, snapshots, preferred_element_type=jnp.float32
    ).astype(jnp.bfloat16)
    point_scale = 1.0 / math.sqrt(points * lax.axis_size("space"))
    shard_count = lax.axis_size("freq") * lax.axis_size("band")
    spectra = lax.all_to_all(spec_local, ("freq", "band"), split_axis=2, concat_axis=0, tiled=True)
    own_points = points // shard_count
    weights_own = lax.dynamic_slice_in_dim(
        weights, lax.axis_index(("freq", "band")) * own_points, own_points
    )
    partial_sums = lax.psum_scatter(
        block_terms(spectra, weights_own, triads, point_scale),
        "space",
        scatter_dimension=0,
        tiled=True,
    )
    result = lax.psum_scatter(partial_sums, ("freq", "band"), scatter_dimension=0, tiled=True)
    return result


def solution(mesh):
    return jax.shard_map(
        per_device,
        mesh=mesh,
        in_specs=(P(("freq", "band"), None, ("groups", "space")), P(("groups", "space")), P()),
        out_specs=P(("groups", "space", "freq", "band"), None),
        check_vma=False,
    )
```

profile of v0, /device:TPU:0, one launch (start us, length us, event | category | flops | bytes accessed | tf_op | source)
XLA Modules:
  0.0 175.1 jit_solution(2965398846534315300)
XLA Ops:
  6.6 0.3 multiply_convert_fusion.2
  6.9 6.6 %fusion.11 = bf16[4,128,4096]{2,1,0:T(8,128)(2,1)} fusion(bf16[4,256,4096]{2,1,0:T(8,128)(2,1)} %param.7, bf16[64,256]{1,0:T(8,128)(2,1)S(1)} %get-tuple-element.80, bf16[64,256]{1,0:T(8,128)(2,1)S(1)} %get-tuple-element.81), kind=kOutput, calls=%fused_computation.35 | convolution fusion | flops 1075970048 | bytes 12648448 | tf_op jit(solution)/shard_map/ct,btx->bcx/dot_general | solution.py:63
  13.5 7.5 %copy.23 = bf16[4,128,4096]{1,0,2:T(4,128)(2,1)} copy(bf16[4,128,4096]{2,1,0:T(8,128)(2,1)} %fusion.11) | data formatting | bytes 8388608 | tf_op jit(solution)/shard_map/convert_element_type | solution.py:65
  21.1 5.0 %all-to-all-start = ((bf16[4,128,4096]{1,0,2:T(4,128)(2,1)}), bf16[4,128,4096]{1,0,2:T(4,128)(2,1)}, u32[]{:S(2)}, u32[]{:S(2)}) async-start(bf16[4,128,4096]{1,0,2:T(4,128)(2,1)} %copy.23), calls=%async_computation | async-start | bytes 8388608 | tf_op jit(solution)/shard_map/all_to_all | solution.py:68
  26.1 0.0 reduce-scatter.2.cloned.1.call-start
  26.1 0.1 reshape.77
  26.2 48.7 %all-to-all-done = bf16[4,128,4096]{1,0,2:T(4,128)(2,1)} async-done(((bf16[4,128,4096]{1,0,2:T(4,128)(2,1)}), bf16[4,128,4096]{1,0,2:T(4,128)(2,1)}, u32[]{:S(2)}, u32[]{:S(2)}) %all-to-all-start) | async-done | bytes 4194336 | tf_op jit(solution)/shard_map/all_to_all | solution.py:68
  74.9 10.0 %copy.24 = bf16[4,4,128,1024]{3,1,0,2:T(4,128)(2,1)} copy(bf16[4,4,128,1024]{2,1,3,0:T(4,128)(2,1)} %bitcast.17) | data formatting | bytes 8388608 | tf_op jit(solution)/shard_map/all_to_all | solution.py:68
  85.0 6.9 %reshape.78 = bf16[16,2,64,1024]{3,0,2,1:T(8,128)(2,1)} reshape(bf16[4,4,128,1024]{3,1,0,2:T(4,128)(2,1)} %copy.24) | data formatting | bytes 8388608 | tf_op jit(solution)/shard_map/reshape | solution.py:49
  91.9 43.5 %while.10 = (s32[]{:T(128)}, f32[2,32,512]{2,1,0:T(8,128)S(1)}, s32[2,32,2]{1,0,2:T(2,128)S(1)}, bf16[16,2,64,1024]{3,0,2,1:T(8,128)(2,1)}, f32[1024]{0:T(1024)S(1)}, /*index=5*/s32[]{:T(128)}) while((s32[]{:T(128)}, f32[2,32,512]{2,1,0:T(8,128)S(1)}, s32[2,32,2]{1,0,2:T(2,128)S(1)}, bf16[16,2,64,1024]{3,0,2,1:T(8,128)(2,1)}, ...), condition=%wide.region_1.3_spmd, body=%wide.region_0.2_spmd.sunk | while | flops 81841760 | bytes 40847500 | solution.py:56
  91.9 2.9 %gather_fusion.1 = bf16[32,16,2,1024]{3,1,2,0:T(8,128)(2,1)S(1)} fusion(bf16[16,2,64,1024]{3,0,2,1:T(8,128)(2,1)} %get-tuple-element.152, s32[1024]{0:T(1024)S(1)} %pad_clamp_fusion.7), kind=kCustom, calls=%fused_computation.1.clone.clone.1 | custom fusion | bytes 4194432 | tf_op jit(solution)/shard_map/while/body/eval_jaxpr/jit(_take)/gather | solution.py:27
  94.8 4.2 %gather_fusion = bf16[32,16,2,1024]{3,1,2,0:T(8,128)(2,1)} fusion(bf16[16,2,64,1024]{3,0,2,1:T(8,128)(2,1)} %get-tuple-element.152, s32[1024]{0:T(1024)S(1)} %pad_clamp_fusion.6), kind=kCustom, calls=%fused_computation.2.clone.clone.1 | custom fusion | bytes 4194432 | tf_op jit(solution)/shard_map/while/body/eval_jaxpr/jit(_take)/gather | solution.py:28
  99.0 2.2 %bitcast_convert_fusion.3 = (f32[16,2,32,1024]{3,0,1,2:T(8,128)S(1)}, f32[16,2,32,1024]{3,0,1,2:T(8,128)S(1)}) fusion(bf16[32,16,2,1024]{3,1,2,0:T(8,128)(2,1)} %gather_fusion, pred[32]{0:T(512)(128)(4,1)S(1)} %get-tuple-element.126, bf16[32,16,2,1024]{3,1,2,0:T(8,128)(2,1)S(1)} %gather_fusion.1, pred[32]{0:T(512)(128)(4,1)S(1)} %get-tuple-element.128), kind=kLoop, calls=%fused_computation.8.clone.1 | loop fusion | flops 4194304 | bytes 12582976 | tf_op jit(solution)/shard_map/while/body/eval_jaxpr/convert_element_type | solution.py:28
  101.2 2.1 %multiply_convert_fusion.5 = (bf16[16,1,32,1024]{3,0,1,2:T(8,128)(2,1)S(1)}, bf16[16,1,32,1024]{3,0,1,2:T(8,128)(2,1)}) fusion(f32[16,2,32,1024]{3,0,1,2:T(8,128)S(1)} %get-tuple-element.129, f32[16,2,32,1024]{3,0,1,2:T(8,128)S(1)} %get-tuple-element.130, f32[1024]{0:T(1024)S(1)} %get-tuple-element.153), kind=kLoop, calls=%fused_computation.12.clone.1 | loop fusion | flops 5242880 | bytes 10489856 | tf_op jit(solution)/shard_map/convert
  103.4 2.9 %gather_fusion.2 = bf16[32,16,2,1024]{3,1,2,0:T(8,128)(2,1)S(1)} fusion(bf16[16,2,64,1024]{3,0,2,1:T(8,128)(2,1)} %get-tuple-element.152, s32[1024]{0:T(1024)S(1)} %pad_clamp_fusion.8), kind=kCustom, calls=%fused_computation.clone.clone.1 | custom fusion | bytes 4194432 | tf_op jit(solution)/shard_map/while/body/eval_jaxpr/jit(_take)/gather | solution.py:29
  106.2 5.4 %fusion.27 = f32[32,16,2,16,2]{3,1,4,2,0:T(8,128)} fusion(bf16[16,1,32,1024]{3,0,1,2:T(8,128)(2,1)} %get-tuple-element.131, bf16[16,1,32,1024]{3,0,1,2:T(8,128)(2,1)S(1)} %get-tuple-element.132, bf16[32,16,2,1024]{3,1,2,0:T(8,128)(2,1)S(1)} %gather_fusion.2, pred[32]{0:T(512)(128)(4,1)S(1)} %get-tuple-element.134), kind=kOutput, calls=%fused_computation.4.clone.1 | convolution fusion | flops 72351744 | bytes 4325408 | tf_op jit(solution)/shard_map/while/body/eval_jaxpr/ictx,jdtx->tcdij/dot_general | solution.py:37
  111.6 1.9 %copy.34 = f32[32,16,2,16,2]{0,1,3,2,4:T(8,128)S(1)} copy(f32[32,16,2,16,2]{3,1,4,2,0:T(8,128)} %fusion.27) | data formatting | bytes 262144 | tf_op jit(solution)/shard_map/while/body/eval_jaxpr/ictx,jdtx->tcdij/dot_general | solution.py:37
  113.5 0.1 copy.35
  113.7 2.9 %gather_fusion.1 = bf16[32,16,2,1024]{3,1,2,0:T(8,128)(2,1)S(1)} fusion(bf16[16,2,64,1024]{3,0,2,1:T(8,128)(2,1)} %get-tuple-element.152, s32[1024]{0:T(1024)S(1)} %pad_clamp_fusion.7), kind=kCustom, calls=%fused_computation.1.clone.clone.1 | custom fusion | bytes 4194432 | tf_op jit(solution)/shard_map/while/body/eval_jaxpr/jit(_take)/gather | solution.py:27
  116.6 4.2 %gather_fusion = bf16[32,16,2,1024]{3,1,2,0:T(8,128)(2,1)} fusion(bf16[16,2,64,1024]{3,0,2,1:T(8,128)(2,1)} %get-tuple-element.152, s32[1024]{0:T(1024)S(1)} %pad_clamp_fusion.6), kind=kCustom, calls=%fused_computation.2.clone.clone.1 | custom fusion | bytes 4194432 | tf_op jit(solution)/shard_map/while/body/eval_jaxpr/jit(_take)/gather | solution.py:28
  120.8 2.2 %bitcast_convert_fusion.3 = (f32[16,2,32,1024]{3,0,1,2:T(8,128)S(1)}, f32[16,2,32,1024]{3,0,1,2:T(8,128)S(1)}) fusion(bf16[32,16,2,1024]{3,1,2,0:T(8,128)(2,1)} %gather_fusion, pred[32]{0:T(512)(128)(4,1)S(1)} %get-tuple-element.126, bf16[32,16,2,1024]{3,1,2,0:T(8,128)(2,1)S(1)} %gather_fusion.1, pred[32]{0:T(512)(128)(4,1)S(1)} %get-tuple-element.128), kind=kLoop, calls=%fused_computation.8.clone.1 | loop fusion | flops 4194304 | bytes 12582976 | tf_op jit(solution)/shard_map/while/body/eval_jaxpr/convert_element_type | solution.py:28
  123.0 2.1 %multiply_convert_fusion.5 = (bf16[16,1,32,1024]{3,0,1,2:T(8,128)(2,1)S(1)}, bf16[16,1,32,1024]{3,0,1,2:T(8,128)(2,1)}) fusion(f32[16,2,32,1024]{3,0,1,2:T(8,128)S(1)} %get-tuple-element.129, f32[16,2,32,1024]{3,0,1,2:T(8,128)S(1)} %get-tuple-element.130, f32[1024]{0:T(1024)S(1)} %get-tuple-element.153), kind=kLoop, calls=%fused_computation.12.clone.1 | loop fusion | flops 5242880 | bytes 10489856 | tf_op jit(solution)/shard_map/convert
  125.2 2.9 %gather_fusion.2 = bf16[32,16,2,1024]{3,1,2,0:T(8,128)(2,1)S(1)} fusion(bf16[16,2,64,1024]{3,0,2,1:T(8,128)(2,1)} %get-tuple-element.152, s32[1024]{0:T(1024)S(1)} %pad_clamp_fusion.8), kind=kCustom, calls=%fused_computation.clone.clone.1 | custom fusion | bytes 4194432 | tf_op jit(solution)/shard_map/while/body/eval_jaxpr/jit(_take)/gather | solution.py:29
  128.0 5.4 %fusion.27 = f32[32,16,2,16,2]{3,1,4,2,0:T(8,128)} fusion(bf16[16,1,32,1024]{3,0,1,2:T(8,128)(2,1)} %get-tuple-element.131, bf16[16,1,32,1024]{3,0,1,2:T(8,128)(2,1)S(1)} %get-tuple-element.132, bf16[32,16,2,1024]{3,1,2,0:T(8,128)(2,1)S(1)} %gather_fusion.2, pred[32]{0:T(512)(128)(4,1)S(1)} %get-tuple-element.134), kind=kOutput, calls=%fused_computation.4.clone.1 | convolution fusion | flops 72351744 | bytes 4325408 | tf_op jit(solution)/shard_map/while/body/eval_jaxpr/ictx,jdtx->tcdij/dot_general | solution.py:37
  133.4 1.9 %copy.34 = f32[32,16,2,16,2]{0,1,3,2,4:T(8,128)S(1)} copy(f32[32,16,2,16,2]{3,1,4,2,0:T(8,128)} %fusion.27) | data formatting | bytes 262144 | tf_op jit(solution)/shard_map/while/body/eval_jaxpr/ictx,jdtx->tcdij/dot_general | solution.py:37
  135.3 0.1 copy.35
  135.5 0.6 copy-done
  136.1 0.0 reduce-scatter.2.cloned.1.call-update
  136.1 0.6 dynamic-slice
  137.4 19.5 %reduce-scatter.2.cloned.1.call-done = f32[16,512]{1,0:T(8,128)} async-done(((f32[64,512]{1,0:T(8,128)}), f32[16,512]{1,0:T(8,128)}) %reduce-scatter.2.cloned.1.call-update) | async-done | bytes 32784 | tf_op jit(solution)/shard_map/reduce_scatter | solution.py:73
  156.8 10.8 %all-reduce = f32[16,512]{1,0:T(8,128)S(1)} all-reduce(f32[16,512]{1,0:T(8,128)} %reduce-scatter.2.cloned.1.call-done), channel_id=3, replica_groups=mesh['groups'=2,'space'=4,'freq'=2,'band'=2] {'freq','band'}, use_global_device_ids=true, to_apply=%region_3.5.clone | all-reduce | flops 8192 | bytes 65536
  167.6 0.6 constant_dynamic-slice_fusion.1
  (26 shorter events, 0.3 us)
Async XLA Ops:
  21.1 5.1 %copy-start.1 = (s32[64,2]{0,1:T(2,128)S(1)}, s32[64,2]{0,1:T(2,128)}, u32[]{:S(2)}) copy-start(s32[64,2]{0,1:T(2,128)} %param.9) | copy-start | bytes 1540
  21.1 53.9 %all-to-all-start = ((bf16[4,128,4096]{1,0,2:T(4,128)(2,1)}), bf16[4,128,4096]{1,0,2:T(4,128)(2,1)}, u32[]{:S(2)}, u32[]{:S(2)}) async-start(bf16[4,128,4096]{1,0,2:T(4,128)(2,1)} %copy.23), calls=%async_computation | async-start | bytes 8388608 | tf_op jit(solution)/shard_map/all_to_all | solution.py:68
  26.1 130.8 %reduce-scatter.2.cloned.1.call-start = ((), (), s32[]{:S(2)}) async-start(), calls=%async_computation.2 | async-start | bytes 163840 | tf_op jit(solution)/shard_map/reduce_scatter | solution.py:73
  85.0 6.9 %dynamic-slice-start = ((f32[4096]{0:T(1024)}, s32[]{:T(128)}), f32[1024]{0:T(1024)S(1)}, s32[]{:S(2)}) async-start(f32[4096]{0:T(1024)} %param.8, s32[]{:T(128)} %select_n.20), calls=%async_computation.3 | async-start | bytes 8704 | tf_op jit(solution)/shard_map/dynamic_slice | solution.py:70
  91.9 44.2 %copy-start.2 = (u32[32]{0:T(128)S(1)}, u32[32]{0:T(128)}, u32[]{:S(2)}) copy-start(u32[32]{0:T(128)} %constant.60) | copy-start | bytes 388
  135.5 0.6 copy-start
Sparse Core Ops, SparseCore 0:
  136.2 20.5 reduce-scatter.1
where the time goes:
time: 176 us; the launch traced here: 175 us
  waiting for transfers between devices  68.2 us (39%)
  local copies, waits for them, and re-layouts  50.2 us (29%)
  matrix products  17.4 us (10%)
  between operations  14.1 us (8%)
  blocking collectives  10.8 us (6%)
  other arithmetic  9.2 us (5%)
  starting transfers between devices  5.01 us (3%)
    all_to_all x1, waiting for transfers between devices, per_device(): lax.all_to_all(spec_local, ('freq', 'band'), split_axis=2, concat_axis=0,...  48.7 us
    reduce_scatter x1, waiting for transfers between devices, per_device(): lax.psum_scatter(block_terms(spectra, weights_own, triads, point_scale),...  19.5 us
    unnamed x1, blocking collectives  10.8 us
    dot_general x2, matrix products, triad_block(): jnp.einsum('ictx,jdtx->tcdij', field_a, third_spec, preferred_element_typ...  10.7 us
    all_to_all x1, local copies, waits for them, and re-layouts, per_device(): lax.all_to_all(spec_local, ('freq', 'band'), split_axis=2, concat_axis=0,...  10 us
    gather x2, local copies, waits for them, and re-layouts, triad_block(): jnp.take(spectra_grid, second_freq, axis=2).astype(jnp.float32)  8.4 us
    convert_element_type x1, local copies, waits for them, and re-layouts, per_device(): spec_local = jnp.einsum('ct,btx->bcx', dft_table, snapshots, preferred_el...  7.54 us
    reshape x1, local copies, waits for them, and re-layouts, block_terms(): spectra_grid = spectra.reshape(NB, 2, NF, columns)  6.92 us
  transfers between devices with their start and end apart: 2, of which 2 were waited for; matrix products, arithmetic and copies ran while one was open for 0% of the time, Pallas kernels for 0%

commit v1 on v0

--- a/solution.py
+++ b/solution.py
@@ -65,7 +65,15 @@
     ).astype(jnp.bfloat16)
     point_scale = 1.0 / math.sqrt(points * lax.axis_size("space"))
     shard_count = lax.axis_size("freq") * lax.axis_size("band")
-    spectra = lax.all_to_all(spec_local, ("freq", "band"), split_axis=2, concat_axis=0, tiled=True)
+    spectra = jnp.concatenate(
+        lax.all_to_all(
+            jnp.stack(jnp.split(spec_local, lax.axis_size(("freq", "band")), axis=2)),
+            ("freq", "band"),
+            0,
+            0,
+        ),
+        axis=0,
+    )
     own_points = points // shard_count
     weights_own = lax.dynamic_slice_in_dim(
         weights, lax.axis_index(("freq", "band")) * own_points, own_points

time: 176 us -> 159 us (0.903)
  local copies, waits for them, and re-layouts: 50.2 us -> 32.6 us
  other arithmetic: 9.2 us -> 11.4 us
  matrix products: 17.4 us -> 15.4 us
    all_to_all x1 -> x0, local copies, waits for them, and re-layouts: 10 us -> none  [per_device(): lax.all_to_all(spec_local, ('freq', 'band'), split_axis=2, concat_axis=0,...]
    convert_element_type x1 -> x0, local copies, waits for them, and re-layouts: 7.54 us -> none  [per_device(): spec_local = jnp.einsum('ct,btx->bcx', dft_table, snapshots, preferred_el...]
    reshape x1 -> x0, local copies, waits for them, and re-layouts: 6.92 us -> none  [block_terms(): spectra_grid = spectra.reshape(NB, 2, NF, columns)]
    while x0 -> x1, local copies, waits for them, and re-layouts: none -> 6.47 us  [block_terms(): result = lax.map(one_group, grouped)]
    another operation x3 -> x4, other arithmetic: 4.52 us -> 6.75 us
    dot_general x1, matrix products: 6.62 us -> 4.66 us  [per_device(): jnp.einsum('ct,btx->bcx', dft_table, snapshots, preferred_element_type=jn...]
where the time goes in v1:
time: 159 us; the launch traced here: 158 us
  waiting for transfers between devices  68.2 us (43%)
  local copies, waits for them, and re-layouts  32.6 us (21%)
  matrix products  15.4 us (10%)
  between operations  14.2 us (9%)
  other arithmetic  11.4 us (7%)
  blocking collectives  10.8 us (7%)
  starting transfers between devices  5.01 us (3%)
    all_to_all x1, waiting for transfers between devices, per_device(): lax.all_to_all(jnp.stack(jnp.split(spec_local, lax.axis_size(('freq', 'ba...  48.7 us
    reduce_scatter x1, waiting for transfers between devices, per_device(): lax.psum_scatter(block_terms(spectra, weights_own, triads, point_scale),...  19.4 us
    unnamed x1, blocking collectives  10.8 us
    dot_general x2, matrix products, triad_block(): jnp.einsum('ictx,jdtx->tcdij', field_a, third_spec, preferred_element_typ...  10.7 us
    gather x2, local copies, waits for them, and re-layouts, triad_block(): jnp.take(spectra_grid, second_freq, axis=2).astype(jnp.float32)  8.39 us
    while x1, local copies, waits for them, and re-layouts, block_terms(): result = lax.map(one_group, grouped)  6.47 us
    gather x2, local copies, waits for them, and re-layouts, triad_block(): first_spec = jnp.take(spectra_grid, first_freq, axis=2).astype(jnp.float32)  5.74 us
    gather x2, local copies, waits for them, and re-layouts, triad_block(): third_spec = jnp.take(spectra_grid, third_freq, axis=2)  5.73 us
  transfers between devices with their start and end apart: 2, of which 2 were waited for; matrix products, arithmetic and copies ran while one was open for 0% of the time, Pallas kernels for 0%

profile of v1, /device:TPU:0, one launch (start us, length us, event | category | flops | bytes accessed | tf_op | source)
XLA Modules:
  0.0 157.8 jit_solution(16919528808621779772)
XLA Ops:
  6.6 0.3 multiply_convert_fusion.2
  6.9 4.7 %fusion.11 = bf16[4,128,4096]{2,1,0:T(8,128)(2,1)S(1)} fusion(bf16[4,256,4096]{2,1,0:T(8,128)(2,1)} %param.7, bf16[64,256]{1,0:T(8,128)(2,1)S(1)} %get-tuple-element.84, bf16[64,256]{1,0:T(8,128)(2,1)S(1)} %get-tuple-element.85), kind=kOutput, calls=%fused_computation.35 | convolution fusion | flops 1075970048 | bytes 12648448 | tf_op jit(solution)/shard_map/ct,btx->bcx/dot_general | solution.py:63
  11.6 0.4 slice_bitcast_fusion.3
  12.0 2.2 %pad_maximum_fusion = bf16[4,4,128,1024]{3,2,1,0:T(8,128)(2,1)} fusion(bf16[1,4,128,1024]{3,2,1,0:T(8,128)(2,1)S(1)} %get-tuple-element.81, bf16[1,4,128,1024]{3,2,1,0:T(8,128)(2,1)S(1)} %get-tuple-element.82, bf16[1,4,128,1024]{3,2,1,0:T(8,128)(2,1)S(1)} %get-tuple-element.83, bf16[1,4,128,1024]{3,2,1,0:T(8,128)(2,1)S(1)} %get-tuple-element.80), kind=kLoop, calls=%fused_computation.36 | loop fusion | flops 6291456 | bytes 8388608 | tf_op jit(solution)/shard_map/stack | solution.py:70
  14.2 5.0 %all-to-all-start = ((bf16[4,4,128,1024]{3,2,1,0:T(8,128)(2,1)}), bf16[4,4,128,1024]{3,2,1,0:T(8,128)(2,1)}, u32[]{:S(2)}, u32[]{:S(2)}) async-start(bf16[4,4,128,1024]{3,2,1,0:T(8,128)(2,1)} %pad_maximum_fusion), calls=%async_computation | async-start | bytes 8388608 | tf_op jit(solution)/shard_map/all_to_all | solution.py:69
  19.2 0.0 reduce-scatter.2.cloned.1.call-start
  19.3 0.1 reshape.73
  19.4 48.7 %all-to-all-done = bf16[4,4,128,1024]{3,2,1,0:T(8,128)(2,1)} async-done(((bf16[4,4,128,1024]{3,2,1,0:T(8,128)(2,1)}), bf16[4,4,128,1024]{3,2,1,0:T(8,128)(2,1)}, u32[]{:S(2)}, u32[]{:S(2)}) %all-to-all-start) | async-done | bytes 4194336 | tf_op jit(solution)/shard_map/all_to_all | solution.py:69
  68.1 6.5 %copy.22 = bf16[16,2,64,1024]{3,0,2,1:T(8,128)(2,1)} copy(bf16[16,2,64,1024]{3,2,1,0:T(8,128)(2,1)} %bitcast.20) | data formatting | bytes 8388608 | tf_op jit(solution)/shard_map/while | solution.py:56
  74.6 43.5 %while.10 = (s32[]{:T(128)}, f32[2,32,512]{2,1,0:T(8,128)S(1)}, s32[2,32,2]{1,0,2:T(2,128)S(1)}, bf16[16,2,64,1024]{3,0,2,1:T(8,128)(2,1)}, f32[1024]{0:T(1024)S(1)}, /*index=5*/s32[]{:T(128)}) while((s32[]{:T(128)}, f32[2,32,512]{2,1,0:T(8,128)S(1)}, s32[2,32,2]{1,0,2:T(2,128)S(1)}, bf16[16,2,64,1024]{3,0,2,1:T(8,128)(2,1)}, ...), condition=%wide.region_1.3_spmd, body=%wide.region_0.2_spmd.sunk | while | flops 81841760 | bytes 40847500 | solution.py:56
  74.7 2.9 %gather_fusion.1 = bf16[32,16,2,1024]{3,1,2,0:T(8,128)(2,1)S(1)} fusion(bf16[16,2,64,1024]{3,0,2,1:T(8,128)(2,1)} %get-tuple-element.156, s32[1024]{0:T(1024)S(1)} %pad_clamp_fusion.7), kind=kCustom, calls=%fused_computation.1.clone.clone.1 | custom fusion | bytes 4194432 | tf_op jit(solution)/shard_map/while/body/eval_jaxpr/jit(_take)/gather | solution.py:27
  77.5 4.2 %gather_fusion = bf16[32,16,2,1024]{3,1,2,0:T(8,128)(2,1)} fusion(bf16[16,2,64,1024]{3,0,2,1:T(8,128)(2,1)} %get-tuple-element.156, s32[1024]{0:T(1024)S(1)} %pad_clamp_fusion.6), kind=kCustom, calls=%fused_computation.2.clone.clone.1 | custom fusion | bytes 4194432 | tf_op jit(solution)/shard_map/while/body/eval_jaxpr/jit(_take)/gather | solution.py:28
  81.7 2.2 %bitcast_convert_fusion.3 = (f32[16,2,32,1024]{3,0,1,2:T(8,128)S(1)}, f32[16,2,32,1024]{3,0,1,2:T(8,128)S(1)}) fusion(bf16[32,16,2,1024]{3,1,2,0:T(8,128)(2,1)} %gather_fusion, pred[32]{0:T(512)(128)(4,1)S(1)} %get-tuple-element.130, bf16[32,16,2,1024]{3,1,2,0:T(8,128)(2,1)S(1)} %gather_fusion.1, pred[32]{0:T(512)(128)(4,1)S(1)} %get-tuple-element.132), kind=kLoop, calls=%fused_computation.8.clone.1 | loop fusion | flops 4194304 | bytes 12582976 | tf_op jit(solution)/shard_map/while/body/eval_jaxpr/convert_element_type | solution.py:28
  83.9 2.1 %multiply_convert_fusion.5 = (bf16[16,1,32,1024]{3,0,1,2:T(8,128)(2,1)S(1)}, bf16[16,1,32,1024]{3,0,1,2:T(8,128)(2,1)}) fusion(f32[16,2,32,1024]{3,0,1,2:T(8,128)S(1)} %get-tuple-element.133, f32[16,2,32,1024]{3,0,1,2:T(8,128)S(1)} %get-tuple-element.134, f32[1024]{0:T(1024)S(1)} %get-tuple-element.157), kind=kLoop, calls=%fused_computation.12.clone.1 | loop fusion | flops 5242880 | bytes 10489856 | tf_op jit(solution)/shard_map/convert
  86.1 2.9 %gather_fusion.2 = bf16[32,16,2,1024]{3,1,2,0:T(8,128)(2,1)S(1)} fusion(bf16[16,2,64,1024]{3,0,2,1:T(8,128)(2,1)} %get-tuple-element.156, s32[1024]{0:T(1024)S(1)} %pad_clamp_fusion.8), kind=kCustom, calls=%fused_computation.clone.clone.1 | custom fusion | bytes 4194432 | tf_op jit(solution)/shard_map/while/body/eval_jaxpr/jit(_take)/gather | solution.py:29
  89.0 5.4 %fusion.27 = f32[32,16,2,16,2]{3,1,4,2,0:T(8,128)} fusion(bf16[16,1,32,1024]{3,0,1,2:T(8,128)(2,1)} %get-tuple-element.135, bf16[16,1,32,1024]{3,0,1,2:T(8,128)(2,1)S(1)} %get-tuple-element.136, bf16[32,16,2,1024]{3,1,2,0:T(8,128)(2,1)S(1)} %gather_fusion.2, pred[32]{0:T(512)(128)(4,1)S(1)} %get-tuple-element.138), kind=kOutput, calls=%fused_computation.4.clone.1 | convolution fusion | flops 72351744 | bytes 4325408 | tf_op jit(solution)/shard_map/while/body/eval_jaxpr/ictx,jdtx->tcdij/dot_general | solution.py:37
  94.3 1.9 %copy.31 = f32[32,16,2,16,2]{0,1,3,2,4:T(8,128)S(1)} copy(f32[32,16,2,16,2]{3,1,4,2,0:T(8,128)} %fusion.27) | data formatting | bytes 262144 | tf_op jit(solution)/shard_map/while/body/eval_jaxpr/ictx,jdtx->tcdij/dot_general | solution.py:37
  96.2 0.1 copy.32
  96.4 2.9 %gather_fusion.1 = bf16[32,16,2,1024]{3,1,2,0:T(8,128)(2,1)S(1)} fusion(bf16[16,2,64,1024]{3,0,2,1:T(8,128)(2,1)} %get-tuple-element.156, s32[1024]{0:T(1024)S(1)} %pad_clamp_fusion.7), kind=kCustom, calls=%fused_computation.1.clone.clone.1 | custom fusion | bytes 4194432 | tf_op jit(solution)/shard_map/while/body/eval_jaxpr/jit(_take)/gather | solution.py:27
  99.3 4.2 %gather_fusion = bf16[32,16,2,1024]{3,1,2,0:T(8,128)(2,1)} fusion(bf16[16,2,64,1024]{3,0,2,1:T(8,128)(2,1)} %get-tuple-element.156, s32[1024]{0:T(1024)S(1)} %pad_clamp_fusion.6), kind=kCustom, calls=%fused_computation.2.clone.clone.1 | custom fusion | bytes 4194432 | tf_op jit(solution)/shard_map/while/body/eval_jaxpr/jit(_take)/gather | solution.py:28
  103.5 2.2 %bitcast_convert_fusion.3 = (f32[16,2,32,1024]{3,0,1,2:T(8,128)S(1)}, f32[16,2,32,1024]{3,0,1,2:T(8,128)S(1)}) fusion(bf16[32,16,2,1024]{3,1,2,0:T(8,128)(2,1)} %gather_fusion, pred[32]{0:T(512)(128)(4,1)S(1)} %get-tuple-element.130, bf16[32,16,2,1024]{3,1,2,0:T(8,128)(2,1)S(1)} %gather_fusion.1, pred[32]{0:T(512)(128)(4,1)S(1)} %get-tuple-element.132), kind=kLoop, calls=%fused_computation.8.clone.1 | loop fusion | flops 4194304 | bytes 12582976 | tf_op jit(solution)/shard_map/while/body/eval_jaxpr/convert_element_type | solution.py:28
  105.7 2.1 %multiply_convert_fusion.5 = (bf16[16,1,32,1024]{3,0,1,2:T(8,128)(2,1)S(1)}, bf16[16,1,32,1024]{3,0,1,2:T(8,128)(2,1)}) fusion(f32[16,2,32,1024]{3,0,1,2:T(8,128)S(1)} %get-tuple-element.133, f32[16,2,32,1024]{3,0,1,2:T(8,128)S(1)} %get-tuple-element.134, f32[1024]{0:T(1024)S(1)} %get-tuple-element.157), kind=kLoop, calls=%fused_computation.12.clone.1 | loop fusion | flops 5242880 | bytes 10489856 | tf_op jit(solution)/shard_map/convert
  107.9 2.9 %gather_fusion.2 = bf16[32,16,2,1024]{3,1,2,0:T(8,128)(2,1)S(1)} fusion(bf16[16,2,64,1024]{3,0,2,1:T(8,128)(2,1)} %get-tuple-element.156, s32[1024]{0:T(1024)S(1)} %pad_clamp_fusion.8), kind=kCustom, calls=%fused_computation.clone.clone.1 | custom fusion | bytes 4194432 | tf_op jit(solution)/shard_map/while/body/eval_jaxpr/jit(_take)/gather | solution.py:29
  110.7 5.4 %fusion.27 = f32[32,16,2,16,2]{3,1,4,2,0:T(8,128)} fusion(bf16[16,1,32,1024]{3,0,1,2:T(8,128)(2,1)} %get-tuple-element.135, bf16[16,1,32,1024]{3,0,1,2:T(8,128)(2,1)S(1)} %get-tuple-element.136, bf16[32,16,2,1024]{3,1,2,0:T(8,128)(2,1)S(1)} %gather_fusion.2, pred[32]{0:T(512)(128)(4,1)S(1)} %get-tuple-element.138), kind=kOutput, calls=%fused_computation.4.clone.1 | convolution fusion | flops 72351744 | bytes 4325408 | tf_op jit(solution)/shard_map/while/body/eval_jaxpr/ictx,jdtx->tcdij/dot_general | solution.py:37
  116.1 1.9 %copy.31 = f32[32,16,2,16,2]{0,1,3,2,4:T(8,128)S(1)} copy(f32[32,16,2,16,2]{3,1,4,2,0:T(8,128)} %fusion.27) | data formatting | bytes 262144 | tf_op jit(solution)/shard_map/while/body/eval_jaxpr/ictx,jdtx->tcdij/dot_general | solution.py:37
  118.0 0.1 copy.32
  118.2 0.6 copy-done
  118.8 0.0 reduce-scatter.2.cloned.1.call-update
  118.8 0.6 dynamic-slice
  120.1 19.4 %reduce-scatter.2.cloned.1.call-done = f32[16,512]{1,0:T(8,128)} async-done(((f32[64,512]{1,0:T(8,128)}), f32[16,512]{1,0:T(8,128)}) %reduce-scatter.2.cloned.1.call-update) | async-done | bytes 32784 | tf_op jit(solution)/shard_map/reduce_scatter | solution.py:81
  139.5 10.8 %all-reduce = f32[16,512]{1,0:T(8,128)S(1)} all-reduce(f32[16,512]{1,0:T(8,128)} %reduce-scatter.2.cloned.1.call-done), channel_id=3, replica_groups=mesh['groups'=2,'space'=4,'freq'=2,'band'=2] {'freq','band'}, use_global_device_ids=true, to_apply=%region_3.5.clone | all-reduce | flops 8192 | bytes 65536
  150.3 0.6 constant_dynamic-slice_fusion.1
  (26 shorter events, 0.3 us)
Async XLA Ops:
  14.2 5.1 %copy-start.1 = (s32[64,2]{0,1:T(2,128)S(1)}, s32[64,2]{0,1:T(2,128)}, u32[]{:S(2)}) copy-start(s32[64,2]{0,1:T(2,128)} %param.9) | copy-start | bytes 1540
  14.2 53.9 %all-to-all-start = ((bf16[4,4,128,1024]{3,2,1,0:T(8,128)(2,1)}), bf16[4,4,128,1024]{3,2,1,0:T(8,128)(2,1)}, u32[]{:S(2)}, u32[]{:S(2)}) async-start(bf16[4,4,128,1024]{3,2,1,0:T(8,128)(2,1)} %pad_maximum_fusion), calls=%async_computation | async-start | bytes 8388608 | tf_op jit(solution)/shard_map/all_to_all | solution.py:69
  19.2 120.3 %reduce-scatter.2.cloned.1.call-start = ((), (), s32[]{:S(2)}) async-start(), calls=%async_computation.2 | async-start | bytes 163840 | tf_op jit(solution)/shard_map/reduce_scatter | solution.py:81
  68.1 6.5 %dynamic-slice-start = ((f32[4096]{0:T(1024)}, s32[]{:T(128)}), f32[1024]{0:T(1024)S(1)}, s32[]{:S(2)}) async-start(f32[4096]{0:T(1024)} %param.8, s32[]{:T(128)} %select_n.20), calls=%async_computation.3 | async-start | bytes 8704 | tf_op jit(solution)/shard_map/dynamic_slice | solution.py:78
  74.6 44.2 %copy-start.2 = (u32[32]{0:T(128)S(1)}, u32[32]{0:T(128)}, u32[]{:S(2)}) copy-start(u32[32]{0:T(128)} %constant.60) | copy-start | bytes 388
  118.2 0.6 copy-start
Sparse Core Ops, SparseCore 0:
  118.9 20.5 reduce-scatter.1
